TPU v7x, 256 devices: a whole 4x4x8 slice. The times are simulated.
256 devices in a mesh: dp: 32 (over x, z_hi, core), tensor: 8 (over y, z_lo).
Axes of the slice: x: 4, y: 4, z: 8 (z_hi: 4, z_lo: 2; z = z_hi * 2 + z_lo), core: 2. Of those that a mesh axis runs over, the one named last changes fastest.
Arguments:
- tokens: bfloat16 [64, 192, 4096], P('dp', None, 'tensor'), may hold values from -6 to 6
- grad_out: bfloat16 [64, 192, 4096], P('dp', None, 'tensor'), may hold values from -6 to 6
- counts: int32 [32], replicated, may hold values from 0 to 2, as said below
- gain: bfloat16 [4096], P('dp'), may hold values from 0.5 to 1.5
- wq: bfloat16 [4096, 4096], P('dp', 'tensor'), may hold values from -2.5 to 2.5
- wk: bfloat16 [4096, 1024], P('dp', 'tensor'), may hold values from -0.09375 to 0.09375
- wv: bfloat16 [4096, 1024], P('dp', 'tensor'), may hold values from -0.09375 to 0.09375
- wo: bfloat16 [4096, 4096], P('tensor', 'dp'), may hold values from -0.09375 to 0.09375
Outputs:
- mixed: bfloat16 [64, 192, 4096], P('dp', None, 'tensor')
- grad_tokens: bfloat16 [64, 192, 4096], P('dp', None, 'tensor')
- grad_gain: float32 [4096], P('dp')
- grad_wq: float32 [4096, 4096], P('dp', 'tensor')
- grad_wk: float32 [4096, 1024], P('dp', 'tensor')
- grad_wv: float32 [4096, 1024], P('dp', 'tensor')
- grad_wo: float32 [4096, 4096], P('tensor', 'dp')
Inputs may be any that keep to these rules, and one draw needn't show every extreme that they name: `counts`: replica r and replica r + 16 hold 2 live blocks together; in every draw some replica holds 2.
All inputs are finite; a program needn't handle non-finite values.
Results may differ from a plain program's by a relative error of at most 0.025.
Values may be sent and summed in bfloat16 or wider, within the bound.
No kernel may reach another device: no remote copies, remote signals or barrier semaphores. Data moves between devices by JAX's collectives and lax.ppermute only.
A program may use at most 128 MiB of HBM per device.

v0:
```python
import jax
import jax.numpy as jnp
from jax import lax
from jax.sharding import PartitionSpec as P

HEADS = 32
KV = 8
HD = 128
epsilon = 1e-05


def attention_forward(query_heads, key_heads, value_heads):
    length = query_heads.shape[1]
    score_scale = query_heads.shape[-1] ** (-0.5)
    position = jnp.arange(length)
    causal = position[None, :] <= position[:, None]
    scores = (
        jnp.einsum("btgrh,bugh->bgrtu", query_heads, key_heads, preferred_element_type=jnp.float32)
        * score_scale
    )
    scores = jnp.where(causal, scores, -1e30)
    row_max = jnp.max(scores, axis=-1, keepdims=True)
    exp_scores = jnp.exp(scores - row_max)
    softmax_out = exp_scores / jnp.sum(exp_scores, axis=-1, keepdims=True)
    softmax_low = softmax_out.astype(jnp.bfloat16)
    context = jnp.einsum(
        "bgrtu,bugh->btgrh", softmax_low, value_heads, preferred_element_type=jnp.float32
    ).astype(jnp.bfloat16)
    return (softmax_out, softmax_low, context)


def attention_backward(grad_context, query_heads, key_heads, value_heads, softmax_out, softmax_low):
    score_scale = query_heads.shape[-1] ** (-0.5)
    grad_soft = jnp.einsum(
        "btgrh,bugh->bgrtu", grad_context, value_heads, preferred_element_type=jnp.float32
    )
    row_inner = jnp.sum(grad_soft * softmax_out, axis=-1, keepdims=True)
    grad_scores = (softmax_out * (grad_soft - row_inner) * score_scale).astype(jnp.bfloat16)
    grad_query = jnp.einsum(
        "bgrtu,bugh->btgrh", grad_scores, key_heads, preferred_element_type=jnp.float32
    ).astype(jnp.bfloat16)
    grad_key = jnp.einsum(
        "bgrtu,btgrh->bugh", grad_scores, query_heads, preferred_element_type=jnp.float32
    ).astype(jnp.bfloat16)
    grad_value = jnp.einsum(
        "bgrtu,btgrh->bugh", softmax_low, grad_context, preferred_element_type=jnp.float32
    ).astype(jnp.bfloat16)
    return (grad_query, grad_key, grad_value)


def on_device(tokens, grad_out, counts, gain, wq, wk, wv, wo):
    groups = lax.axis_size("tensor")
    dp_size = lax.axis_size("dp")
    replica = lax.axis_index("dp")
    own_count = counts[replica]
    blocks, length, shard_width = tokens.shape
    full_width = shard_width * groups
    d_local = gain.shape[0]
    q_cols = wq.shape[1]
    k_cols = wk.shape[1]
    o_rows = wo.shape[0]
    lane = wo.shape[1]
    pack = jnp.concatenate(
        [
            jnp.pad(gain.reshape(1, d_local), ((0, 7), (0, 0))),
            wq.reshape(d_local * q_cols // lane, lane),
            wk.reshape(d_local * k_cols // lane, lane),
            wv.reshape(d_local * k_cols // lane, lane),
            wo,
        ],
        axis=0,
    )
    packed = lax.all_gather(pack, "dp", axis=0, tiled=False)
    r0 = 8
    r1 = r0 + d_local * q_cols // lane
    r2 = r1 + d_local * k_cols // lane
    r3 = r2 + d_local * k_cols // lane
    r4 = r3 + o_rows
    gain_all = packed[:, 0, :].reshape(full_width)
    wq_all = packed[:, r0:r1, :].reshape(dp_size * d_local, q_cols)
    wk_all = packed[:, r1:r2, :].reshape(dp_size * d_local, k_cols)
    wv_all = packed[:, r2:r3, :].reshape(dp_size * d_local, k_cols)
    wo_blk = packed[:, r3:r4, :]
    live_mask = (jnp.arange(blocks) < own_count).astype(jnp.bfloat16)[:, None, None]
    block_grad = grad_out * live_mask
    both = lax.all_gather(jnp.stack([tokens, block_grad]), "tensor", axis=3, tiled=True)
    wide_in, upstream = (both[0], both[1])
    repeat = HEADS // KV
    kv_local = wk_all.shape[1] // HD
    wide_float = wide_in.astype(jnp.float32)
    inverse_rms = lax.rsqrt(jnp.mean(wide_float * wide_float, axis=-1, keepdims=True) + epsilon)
    unit_rows = wide_float * inverse_rms
    gain_float = gain_all.astype(jnp.float32)
    normed_float = unit_rows * gain_float
    normed = normed_float.astype(jnp.bfloat16)
    queries = jnp.einsum("btd,dk->btk", normed, wq_all, preferred_element_type=jnp.float32).astype(
        jnp.bfloat16
    )
    key_rows = jnp.einsum("btd,dk->btk", normed, wk_all, preferred_element_type=jnp.float32).astype(
        jnp.bfloat16
    )
    values = jnp.einsum("btd,dk->btk", normed, wv_all, preferred_element_type=jnp.float32).astype(
        jnp.bfloat16
    )
    query_heads = queries.reshape(blocks, length, kv_local, repeat, HD)
    key_heads = key_rows.reshape(blocks, length, kv_local, HD)
    value_heads = values.reshape(blocks, length, kv_local, HD)
    softmax_out, softmax_low, context = attention_forward(query_heads, key_heads, value_heads)
    context_flat = context.reshape(blocks, length, kv_local * repeat * HD)
    partial_value = jnp.einsum(
        "btk,jkl->btjl", context_flat, wo_blk, preferred_element_type=jnp.float32
    ).reshape(blocks, length, full_width)
    upstream_blk = upstream.reshape(blocks, length, dp_size, lane)
    grad_context = jnp.einsum(
        "btjl,jkl->btk", upstream_blk, wo_blk, preferred_element_type=jnp.float32
    ).astype(jnp.bfloat16)
    grad_output_proj = jnp.einsum(
        "btk,btjl->jkl", context_flat, upstream_blk, preferred_element_type=jnp.float32
    )
    grad_query, grad_key, grad_value = attention_backward(
        grad_context.reshape(blocks, length, kv_local, repeat, HD),
        query_heads,
        key_heads,
        value_heads,
        softmax_out,
        softmax_low,
    )
    grad_query = grad_query.reshape(blocks, length, -1)
    grad_key = grad_key.reshape(blocks, length, -1)
    grad_value = grad_value.reshape(blocks, length, -1)
    normed_terms = jnp.einsum("btk,dk->btd", grad_query, wq_all, preferred_element_type=jnp.float32)
    normed_terms = normed_terms + jnp.einsum(
        "btk,dk->btd", grad_key, wk_all, preferred_element_type=jnp.float32
    )
    normed_terms = normed_terms + jnp.einsum(
        "btk,dk->btd", grad_value, wv_all, preferred_element_type=jnp.float32
    )
    grad_query_proj = jnp.einsum(
        "btd,btk->dk", normed, grad_query, preferred_element_type=jnp.float32
    )
    grad_key_proj = jnp.einsum("btd,btk->dk", normed, grad_key, preferred_element_type=jnp.float32)
    grad_value_proj = jnp.einsum(
        "btd,btk->dk", normed, grad_value, preferred_element_type=jnp.float32
    )
    term_low = normed_terms.astype(jnp.bfloat16)
    term_float = term_low.astype(jnp.float32)
    rows = blocks * length
    row_dot = jnp.sum(term_float * normed_float, axis=-1).reshape(rows)
    gain_part = jnp.sum(term_float * unit_rows, axis=(0, 1))
    extra_rows = 1 + full_width // shard_width
    extra = jnp.concatenate(
        [
            jnp.pad(row_dot, (0, shard_width - rows)).reshape(1, shard_width),
            gain_part.reshape(full_width // shard_width, shard_width),
        ],
        axis=0,
    )
    extra_pad = -extra_rows % 8
    extra = jnp.pad(extra, ((0, extra_pad), (0, 0))).astype(jnp.bfloat16)

    def by_chunk(x):
        return x.reshape(rows, groups, shard_width).transpose(1, 0, 2)

    payload = jnp.concatenate(
        [
            by_chunk(partial_value.astype(jnp.bfloat16)),
            by_chunk(term_low),
            jnp.broadcast_to(extra[None], (groups,) + extra.shape),
        ],
        axis=1,
    )
    reduced = lax.psum_scatter(payload, "tensor", scatter_dimension=0, tiled=True)[0]
    reduced = reduced.astype(jnp.float32)
    attn_sum = reduced[:rows].reshape(blocks, length, shard_width)
    grad_normed = reduced[rows : 2 * rows].reshape(blocks, length, shard_width)
    row_mean = (reduced[2 * rows, :rows] / full_width).reshape(blocks, length, 1)
    gain_term = reduced[2 * rows + 1 : 2 * rows + extra_rows].reshape(full_width)
    mixed_block = ((tokens.astype(jnp.float32) + attn_sum) * live_mask.astype(jnp.float32)).astype(
        jnp.bfloat16
    )
    shard_start = lax.axis_index("tensor") * shard_width
    own_unit = lax.dynamic_slice_in_dim(unit_rows, shard_start, shard_width, 2)
    own_gain = lax.dynamic_slice_in_dim(gain_float, shard_start, shard_width, 0)
    own_grad = inverse_rms * (grad_normed * own_gain - own_unit * row_mean)
    grad_block = (block_grad.astype(jnp.float32) + own_grad).astype(jnp.bfloat16)
    gpack = jnp.concatenate(
        [
            jnp.pad(gain_term.reshape(dp_size, 1, d_local), ((0, 0), (0, 7), (0, 0))),
            grad_query_proj.reshape(dp_size, d_local * q_cols // lane, lane),
            grad_key_proj.reshape(dp_size, d_local * k_cols // lane, lane),
            grad_value_proj.reshape(dp_size, d_local * k_cols // lane, lane),
            grad_output_proj,
        ],
        axis=1,
    ).astype(jnp.bfloat16)
    greduced = lax.psum_scatter(gpack, "dp", scatter_dimension=0, tiled=True)[0].astype(jnp.float32)
    grad_gain = greduced[0]
    grad_wq = greduced[r0:r1].reshape(d_local, q_cols)
    grad_wk = greduced[r1:r2].reshape(d_local, k_cols)
    grad_wv = greduced[r2:r3].reshape(d_local, k_cols)
    grad_wo = greduced[r3:r4]
    return (mixed_block, grad_block, grad_gain, grad_wq, grad_wk, grad_wv, grad_wo)


def solution(mesh):
    return jax.shard_map(
        on_device,
        mesh=mesh,
        in_specs=(
            P("dp", None, "tensor"),
            P("dp", None, "tensor"),
            P(),
            P("dp"),
            P("dp", "tensor"),
            P("dp", "tensor"),
            P("dp", "tensor"),
            P("tensor", "dp"),
        ),
        out_specs=(
            P("dp", None, "tensor"),
            P("dp", None, "tensor"),
            P("dp"),
            P("dp", "tensor"),
            P("dp", "tensor"),
            P("dp", "tensor"),
            P("tensor", "dp"),
        ),
        check_vma=False,
    )
```

profile of v0, /device:TPU:1, one launch (start us, length us, event | category | flops | bytes accessed | tf_op | source)
XLA Modules:
  0.0 626.7 jit_solution(15260371974625475414)
XLA Ops:
  14.0 134.4 %all-gather.4.cloned.1.call-done = bf16[2,2,192,4096]{3,2,1,0:T(8,128)(2,1)} async-done(((bf16[2,2,192,512]{3,2,1,0:T(8,128)(2,1)}), bf16[2,2,192,4096]{3,2,1,0:T(8,128)(2,1)}) %all-gather.4.cloned.1.call-update) | async-done | bytes 6291472 | tf_op jit(solution)/shard_map/all_gather | solution.py:86
  150.3 2.5 copy.68
  154.9 87.3 %all-gather.6.cloned.1.call-done = bf16[41216,128]{1,0:T(8,128)(2,1)} async-done(((bf16[1288,128]{1,0:T(8,128)(2,1)}), bf16[41216,128]{1,0:T(8,128)(2,1)}) %all-gather.6.cloned.1.call-update) | async-done | bytes 10551312 | tf_op jit(solution)/shard_map/all_gather | solution.py:73
  244.8 6.6 %slice_bitcast_fusion = (bf16[32,128,512]{1,2,0:T(8,128)(2,1)}, bf16[32,512,128]{2,1,0:T(8,128)(2,1)}) fusion(bf16[32,1288,128]{2,1,0:T(8,128)(2,1)} %bitcast.235), kind=kLoop, calls=%fused_computation.21 | loop fusion | bytes 16777216 | tf_op jit(solution)/shard_map/btk,jkl->btjl/dot_general | solution.py:110
  251.4 4.2 fusion.44
  255.6 7.5 %reshape.219 = bf16[4096,512,1]{1,0,2:T(8,128)(2,1)} reshape(bf16[32,512,128]{2,1,0:T(8,128)(2,1)} %get-tuple-element.24) | data formatting | bytes 8388608 | tf_op jit(solution)/shard_map/reshape | solution.py:80
  263.1 3.1 fusion.52
  266.3 4.0 fusion.43
  275.5 7.0 %copy.34 = bf16[32,128,512]{2,1,0:T(8,128)(2,1)} copy(bf16[32,128,512]{1,2,0:T(8,128)(2,1)} %get-tuple-element.23) | data formatting | bytes 8388608 | tf_op jit(solution)/shard_map/btk,jkl->btjl/dot_general | solution.py:110
  282.9 4.0 convolution_convert_fusion
  287.0 3.2 copy.67
  290.6 4.1 fusion.86
  298.2 6.0 fusion.5
  312.3 6.2 pad_maximum_fusion
  319.5 6.5 %bitcast_convert_fusion.1 = bf16[4096,512]{1,0:T(8,128)(2,1)} fusion(bf16[2,192,512]{2,1,0:T(8,128)(2,1)S(1)} %copy-done.14, f32[4096]{0:T(1024)S(1)} %bitcast.250, f32[2,192]{1,0:T(2,128)S(1)} %copy-done.27, bf16[2,2,192,4096]{3,2,1,0:T(8,128)(2,1)} %all-gather.4.cloned.1.call-done), kind=kOutput, calls=%fused_computation.1 | convolution fusion | flops 1619001344 | bytes 7751168 | tf_op jit(solution)/shard_map/btd,btk->dk/dot_general | solution.py:138
  326.0 7.9 %reshape.212 = bf16[32,512,128]{2,1,0:T(8,128)(2,1)} reshape(bf16[4096,512]{1,0:T(8,128)(2,1)} %bitcast_convert_fusion.1) | data formatting | bytes 8388608 | tf_op jit(solution)/shard_map/reshape | solution.py:189
  333.9 6.6 %copy.47 = bf16[32,512,128]{1,2,0:T(8,128)(2,1)} copy(bf16[32,512,128]{2,1,0:T(8,128)(2,1)} %reshape.212) | data formatting | bytes 8388608 | tf_op jit(solution)/shard_map/reshape | solution.py:189
  342.5 2.3 copy.48
  344.8 4.1 bitcast_convert_fusion.2
  351.2 4.7 fusion.7
  355.8 95.5 %reduce-scatter.3.cloned.1.call-done = bf16[1,784,512]{2,1,0:T(8,128)(2,1)} async-done(((bf16[8,784,512]{2,1,0:T(8,128)(2,1)}), bf16[1,784,512]{2,1,0:T(8,128)(2,1)}) %reduce-scatter.3.cloned.1.call-update) | async-done | bytes 802832 | tf_op jit(solution)/shard_map/reduce_scatter | solution.py:172
  452.0 3.2 reshape_reshape.5
  456.7 19.6 %concatenate.17 = bf16[32,1288,128]{1,2,0:T(8,128)(2,1)} concatenate(bf16[32,8,128]{1,2,0:T(8,128)(2,1)S(1)} %pad.22, bf16[32,512,128]{1,2,0:T(8,128)(2,1)} %copy.47, bf16[32,128,128]{1,2,0:T(8,128)(2,1)S(1)} %copy-done.6, bf16[32,128,128]{1,2,0:T(8,128)(2,1)S(1)} %copy-done.7, bf16[32,512,128]{1,2,0:T(8,128)(2,1)} %fusion.7), dimensions={1} | concatenate | bytes 21102592 | tf_op jit(solution)/shard_map/concatenate | solution.py:186
  481.1 132.7 %reduce-scatter.5.cloned.1.call-done = bf16[1,1288,128]{1,2,0:T(8,128)(2,1)} async-done(((bf16[32,1288,128]{1,2,0:T(8,128)(2,1)}), bf16[1,1288,128]{1,2,0:T(8,128)(2,1)}) %reduce-scatter.5.cloned.1.call-update) | async-done | bytes 329744 | tf_op jit(solution)/shard_map/reduce_scatter | solution.py:196
  (147 shorter events, 49.0 us)
Async XLA Ops:
  7.2 5.8 copy-start.19
  7.2 5.9 copy-start.32
  7.2 5.9 copy-start.22
  7.2 5.9 copy-start.23
  7.2 5.9 copy-start.20
  7.2 141.2 %all-gather.4.cloned.1.call-start = ((), (), s32[]{:S(2)}) async-start(), calls=%async_computation.2 | async-start | bytes 7077888 | tf_op jit(solution)/shard_map/all_gather | solution.py:86
  12.9 229.4 %all-gather.6.cloned.1.call-start = ((), (), s32[]{:S(2)}) async-start(), calls=%async_computation.5 | async-start | bytes 10881024 | tf_op jit(solution)/shard_map/all_gather | solution.py:73
  13.9 437.4 %reduce-scatter.3.cloned.1.call-start = ((), (), s32[]{:S(2)}) async-start(), calls=%async_computation.3 | async-start | bytes 7225344 | tf_op jit(solution)/shard_map/reduce_scatter | solution.py:172
  150.3 3.9 copy-start.1
  154.9 117.2 %copy-start.25 = (f32[2,192]{1,0:T(2,128)}, f32[2,192]{1,0:T(2,128)S(1)}, u32[]{:S(2)}) copy-start(f32[2,192]{1,0:T(2,128)S(1)} %add_rsqrt_fusion) | copy-start | bytes 4612
  244.8 27.3 %copy-start.8 = (bf16[32,128,128]{2,1,0:T(8,128)(2,1)}, bf16[32,128,128]{2,1,0:T(8,128)(2,1)S(1)}, u32[]{:S(2)}) copy-start(bf16[32,128,128]{2,1,0:T(8,128)(2,1)S(1)} %get-tuple-element.25) | copy-start | bytes 3145732
  244.8 6.6 %copy-start.2 = (bf16[48,8,32,128]{3,2,1,0:T(8,128)(2,1)S(1)}, bf16[48,8,32,128]{3,2,1,0:T(8,128)(2,1)}, u32[]{:S(2)}) copy-start(bf16[48,8,32,128]{3,2,1,0:T(8,128)(2,1)} %copy.68) | copy-start | bytes 9437188
  263.1 3.1 copy-start
  263.1 8.9 %slice-start = ((s8[6291456]{0:T(1024)(128)(4,1)}), s8[4194304]{0:T(1024)(128)(4,1)S(1)}, s32[]{:S(2)}) async-start(s8[6291456]{0:T(1024)(128)(4,1)} %bitcast.224), calls=%async_computation.6 | async-start | bytes 8388608
  266.3 5.8 slice-start.1
  275.0 19.8 %copy-start.16 = (bf16[2,128,192]{1,2,0:T(8,128)(2,1)}, bf16[2,128,192]{1,2,0:T(8,128)(2,1)S(1)}, u32[]{:S(2)}) copy-start(bf16[2,128,192]{1,2,0:T(8,128)(2,1)S(1)} %fusion.49) | copy-start | bytes 294916
  290.6 4.2 copy-start.13
  318.5 295.3 %reduce-scatter.5.cloned.1.call-start = ((), (), s32[]{:S(2)}) async-start(), calls=%async_computation.4 | async-start | bytes 11894784 | tf_op jit(solution)/shard_map/reduce_scatter | solution.py:196
  333.9 6.6 %copy-start.10 = (bf16[2,24,32,8,128]{4,3,2,1,0:T(8,128)(2,1)S(1)}, bf16[2,24,32,8,128]{4,3,2,1,0:T(8,128)(2,1)}, u32[]{:S(2)}) copy-start(bf16[2,24,32,8,128]{4,3,2,1,0:T(8,128)(2,1)} %get-tuple-element.27) | copy-start | bytes 9437188
  333.9 6.6 %copy-start.17 = (bf16[2,128,192]{1,2,0:T(8,128)(2,1)S(1)}, bf16[2,128,192]{1,2,0:T(8,128)(2,1)}, u32[]{:S(2)}) copy-start(bf16[2,128,192]{1,2,0:T(8,128)(2,1)} %copy-done.16) | copy-start | bytes 294916
  344.8 6.3 %copy-start.3 = (bf16[48,8,32,128]{3,2,1,0:T(8,128)(2,1)S(1)}, bf16[48,8,32,128]{3,2,1,0:T(8,128)(2,1)}, u32[]{:S(2)}) copy-start(bf16[48,8,32,128]{3,2,1,0:T(8,128)(2,1)} %copy.68) | copy-start | bytes 9437188
  344.8 6.3 %copy-start.15 = (bf16[2,192,512,1]{2,1,0,3:T(8,128)(2,1)S(1)}, bf16[2,192,512,1]{2,1,0,3:T(8,128)(2,1)}, u32[]{:S(2)}) copy-start(bf16[2,192,512,1]{2,1,0,3:T(8,128)(2,1)} %reshape.232) | copy-start | bytes 1179652
  355.8 100.9 %copy-start.6 = (bf16[32,128,128]{1,2,0:T(8,128)(2,1)S(1)}, bf16[32,128,128]{1,2,0:T(8,128)(2,1)}, u32[]{:S(2)}) copy-start(bf16[32,128,128]{1,2,0:T(8,128)(2,1)} %copy.48) | copy-start | bytes 3145732
  355.8 100.9 %copy-start.7 = (bf16[32,128,128]{1,2,0:T(8,128)(2,1)S(1)}, bf16[32,128,128]{1,2,0:T(8,128)(2,1)}, u32[]{:S(2)}) copy-start(bf16[32,128,128]{1,2,0:T(8,128)(2,1)} %copy.49) | copy-start | bytes 3145732
  (18 other events, 26.5 us)
Sparse Core Ops, SparseCore 0:
  13.0 135.3 all-gather.3
  151.6 90.6 all-gather.5
  318.7 132.6 reduce-scatter.2
  476.5 137.2 reduce-scatter.4
where the time goes:
time: 637 us; the launch traced here: 627 us
  waiting for transfers between devices  450 us (71%)
  local copies, waits for them, and re-layouts  95.7 us (15%)
  matrix products  43 us (7%)
  other arithmetic  23.3 us (4%)
  between operations  14.5 us (2%)
    all_gather x1, waiting for transfers between devices, on_device(): lax.all_gather(jnp.stack([tokens, block_grad]), 'tensor', axis=3, tiled=T...  134 us
    reduce_scatter x1, waiting for transfers between devices, on_device(): lax.psum_scatter(gpack, 'dp', scatter_dimension=0, tiled=True)[0]  133 us
    reduce_scatter x1, waiting for transfers between devices, on_device(): lax.psum_scatter(payload, 'tensor', scatter_dimension=0, tiled=True)[0]  95.5 us
    all_gather x1, waiting for transfers between devices, on_device(): packed = lax.all_gather(pack, 'dp', axis=0, tiled=False)  87.3 us
    concatenate x1, local copies, waits for them, and re-layouts, on_device(): jnp.concatenate([jnp.pad(gain_term.reshape(dp_size, 1, d_local), ((0, 0),...  19.6 us
    reshape x2, local copies, waits for them, and re-layouts, on_device(): grad_query_proj.reshape(dp_size, d_local * q_cols // lane, lane)  14.5 us
    unnamed x84, local copies, waits for them, and re-layouts  14.5 us
    dot_general x2, local copies, waits for them, and re-layouts, on_device(): jnp.einsum('btk,jkl->btjl', context_flat, wo_blk, preferred_element_type=...  13.5 us
  transfers between devices with their start and end apart: 4, of which 4 were waited for; matrix products, arithmetic and copies ran while one was open for 7% of the time, Pallas kernels for 0%

commit v1 on v0

--- a/solution.py
+++ b/solution.py
@@ -83,7 +83,12 @@
     wo_blk = packed[:, r3:r4, :]
     live_mask = (jnp.arange(blocks) < own_count).astype(jnp.bfloat16)[:, None, None]
     block_grad = grad_out * live_mask
-    both = lax.all_gather(jnp.stack([tokens, block_grad]), "tensor", axis=3, tiled=True)
+    both = jnp.concatenate(
+        lax.all_to_all(
+            jnp.stack([jnp.stack([tokens, block_grad])] * lax.axis_size("tensor")), "tensor", 0, 0
+        ),
+        axis=3,
+    )
     wide_in, upstream = (both[0], both[1])
     repeat = HEADS // KV
     kv_local = wk_all.shape[1] // HD

time: 637 us -> 597 us (0.937)
  waiting for transfers between devices: 450 us -> 356 us
  local copies, waits for them, and re-layouts: 95.7 us -> 131 us
  other arithmetic: 23.3 us -> 33.3 us
    all_gather x1 -> x0, waiting for transfers between devices: 134 us -> none  [on_device(): lax.all_gather(jnp.stack([tokens, block_grad]), 'tensor', axis=3, tiled=T...]
    all_to_all x0 -> x1, waiting for transfers between devices: none -> 124 us  [on_device(): lax.all_to_all(jnp.stack([jnp.stack([tokens, block_grad])] * lax.axis_siz...]
    all_gather x1, waiting for transfers between devices: 87.3 us -> 0.02 us  [on_device(): packed = lax.all_gather(pack, 'dp', axis=0, tiled=False)]
    convert_element_type x0 -> x5, local copies, waits for them, and re-layouts: none -> 21.5 us  [the longest x2 13.9 us: on_device(): wide_float = wide_in.astype(jnp.float32)]
    convert_element_type x0 -> x2, other arithmetic: none -> 8.34 us  [the longest x1 5.56 us: on_device(): wide_float = wide_in.astype(jnp.float32)]
    another operation x2 -> x4, local copies, waits for them, and re-layouts: 4.55 us -> 11.8 us
    unnamed x84 -> x61, local copies, waits for them, and re-layouts: 14.5 us -> 13.3 us
  transfers between devices with their start and end apart: 4 -> 4, of which waited for: 4 -> 3; matrix products, arithmetic and copies ran while one was open for 7% -> 13% of each run, Pallas kernels for 0% -> 0%
where the time goes in v1:
time: 597 us; the launch traced here: 590 us
  waiting for transfers between devices  356 us (60%)
  local copies, waits for them, and re-layouts  131 us (22%)
  matrix products  48.4 us (8%)
  other arithmetic  33.3 us (6%)
  between operations  14.5 us (2%)
  starting transfers between devices  6.48 us (1%)
    reduce_scatter x1, waiting for transfers between devices, on_device(): lax.psum_scatter(gpack, 'dp', scatter_dimension=0, tiled=True)[0]  133 us
    all_to_all x1, waiting for transfers between devices, on_device(): lax.all_to_all(jnp.stack([jnp.stack([tokens, block_grad])] * lax.axis_siz...  124 us
    reduce_scatter x1, waiting for transfers between devices, on_device(): lax.psum_scatter(payload, 'tensor', scatter_dimension=0, tiled=True)[0]  99.5 us
    concatenate x1, local copies, waits for them, and re-layouts, on_device(): jnp.concatenate([jnp.pad(gain_term.reshape(dp_size, 1, d_local), ((0, 0),...  19.6 us
    reshape x2, local copies, waits for them, and re-layouts, on_device(): grad_query_proj.reshape(dp_size, d_local * q_cols // lane, lane)  14.3 us
    convert_element_type x2, local copies, waits for them, and re-layouts, on_device(): wide_float = wide_in.astype(jnp.float32)  13.9 us
    unnamed x61, local copies, waits for them, and re-layouts  13.3 us
    dot_general x2, local copies, waits for them, and re-layouts, on_device(): jnp.einsum('btk,jkl->btjl', context_flat, wo_blk, preferred_element_type=...  12.4 us
  transfers between devices with their start and end apart: 4, of which 3 were waited for; matrix products, arithmetic and copies ran while one was open for 13% of the time, Pallas kernels for 0%

profile of v1, /device:TPU:1, one launch (start us, length us, event | category | flops | bytes accessed | tf_op | source)
XLA Modules:
  0.0 589.6 jit_solution(17397916263425329936)
XLA Ops:
  19.5 6.4 %all-to-all-start = ((bf16[8,2,2,192,512]{4,3,2,1,0:T(8,128)(2,1)}), bf16[8,2,2,192,512]{4,3,2,1,0:T(8,128)(2,1)}, u32[]{:S(2)}, u32[]{:S(2)}) async-start(bf16[8,2,2,192,512]{4,3,2,1,0:T(8,128)(2,1)} %stack.11), calls=%async_computation | async-start | bytes 12582912 | tf_op jit(solution)/shard_map/all_to_all | solution.py:87
  26.0 123.5 %all-to-all-done = bf16[8,2,2,192,512]{4,3,2,1,0:T(8,128)(2,1)} async-done(((bf16[8,2,2,192,512]{4,3,2,1,0:T(8,128)(2,1)}), bf16[8,2,2,192,512]{4,3,2,1,0:T(8,128)(2,1)}, u32[]{:S(2)}, u32[]{:S(2)}) %all-to-all-start) | async-done | bytes 6291488 | tf_op jit(solution)/shard_map/all_to_all | solution.py:87
  149.5 5.6 slice_convert_fusion
  155.0 6.3 %copy.93 = f32[1,2,192,8,512]{4,3,2,1,0:T(8,128)} copy(f32[1,2,192,8,512]{4,2,1,0,3:T(8,128)S(1)} %get-tuple-element.43) | data formatting | bytes 12582912 | tf_op jit(solution)/shard_map/convert_element_type | solution.py:95
  161.3 7.7 %reshape.237 = f32[2,192,4096]{2,1,0:T(8,128)} reshape(f32[1,2,192,8,512]{4,3,2,1,0:T(8,128)} %copy.93) | data formatting | bytes 12582912 | tf_op jit(solution)/shard_map/convert_element_type | solution.py:95
  183.9 5.9 %slice_bitcast_fusion = (bf16[32,128,512]{1,2,0:T(8,128)(2,1)}, bf16[32,512,128]{2,1,0:T(8,128)(2,1)}) fusion(bf16[32,1288,128]{2,1,0:T(8,128)(2,1)} %bitcast.215), kind=kLoop, calls=%fused_computation.16 | loop fusion | bytes 16777216 | tf_op jit(solution)/shard_map/btk,jkl->btjl/dot_general | solution.py:115
  196.0 4.2 convert_element_type.159
  204.4 5.0 fusion.38
  209.3 7.7 %reshape.242 = bf16[4096,512,1]{1,0,2:T(8,128)(2,1)} reshape(bf16[32,512,128]{2,1,0:T(8,128)(2,1)} %get-tuple-element.40) | data formatting | bytes 8388608 | tf_op jit(solution)/shard_map/reshape | solution.py:80
  217.0 4.0 fusion.37
  227.5 6.5 %copy.83 = bf16[32,128,512]{2,1,0:T(8,128)(2,1)} copy(bf16[32,128,512]{1,2,0:T(8,128)(2,1)} %get-tuple-element.39) | data formatting | bytes 8388608 | tf_op jit(solution)/shard_map/btk,jkl->btjl/dot_general | solution.py:115
  236.2 4.1 convolution_convert_fusion
  246.4 4.2 fusion.77
  251.6 5.8 fusion.6
  257.5 4.5 fusion
  271.7 6.2 %pad_maximum_fusion = bf16[8,784,512]{2,1,0:T(8,128)(2,1)} fusion(bf16[8,16,512]{2,1,0:T(8,128)(2,1)S(1)} %broadcast_in_dim.12, bf16[8,384,512]{2,1,0:T(8,128)(2,1)S(1)} %get-tuple-element.54, bf16[8,384,512]{2,1,0:T(8,128)(2,1)S(1)} %get-tuple-element.55), kind=kLoop, calls=%fused_computation.4 | loop fusion | flops 19267584 | bytes 12845056 | tf_op jit(solution)/shard_map/concatenate | solution.py:169
  285.3 4.0 bitcast_convert_fusion.3
  291.5 4.4 bitcast_convert_fusion.1
  295.9 7.6 %reshape.234 = bf16[32,512,128]{2,1,0:T(8,128)(2,1)} reshape(bf16[4096,512]{1,0:T(8,128)(2,1)} %bitcast_convert_fusion.1) | data formatting | bytes 8388608 | tf_op jit(solution)/shard_map/reshape | solution.py:194
  303.6 6.6 %copy.98 = bf16[32,512,128]{1,2,0:T(8,128)(2,1)} copy(bf16[32,512,128]{2,1,0:T(8,128)(2,1)} %reshape.234) | data formatting | bytes 8388608 | tf_op jit(solution)/shard_map/reshape | solution.py:194
  310.2 4.7 fusion.2
  314.9 99.5 %reduce-scatter.3.cloned.1.call-done = bf16[1,784,512]{2,1,0:T(8,128)(2,1)} async-done(((bf16[8,784,512]{2,1,0:T(8,128)(2,1)}), bf16[1,784,512]{2,1,0:T(8,128)(2,1)}) %reduce-scatter.3.cloned.1.call-update) | async-done | bytes 802832 | tf_op jit(solution)/shard_map/reduce_scatter | solution.py:177
  419.8 19.6 %concatenate.17 = bf16[32,1288,128]{1,2,0:T(8,128)(2,1)} concatenate(bf16[32,8,128]{1,2,0:T(8,128)(2,1)S(1)} %pad.22, bf16[32,512,128]{1,2,0:T(8,128)(2,1)} %copy.98, bf16[32,128,128]{1,2,0:T(8,128)(2,1)S(1)} %copy-done.9, bf16[32,128,128]{1,2,0:T(8,128)(2,1)S(1)} %copy-done.8, bf16[32,512,128]{1,2,0:T(8,128)(2,1)} %fusion.2), dimensions={1} | concatenate | bytes 21102592 | tf_op jit(solution)/shard_map/concatenate | solution.py:191
  444.2 132.6 %reduce-scatter.5.cloned.1.call-done = bf16[1,1288,128]{1,2,0:T(8,128)(2,1)} async-done(((bf16[32,1288,128]{1,2,0:T(8,128)(2,1)}), bf16[1,1288,128]{1,2,0:T(8,128)(2,1)}) %reduce-scatter.5.cloned.1.call-update) | async-done | bytes 329744 | tf_op jit(solution)/shard_map/reduce_scatter | solution.py:201
  (130 shorter events, 88.7 us)
Async XLA Ops:
  7.2 171.8 %all-gather.3.cloned.1.call-start = ((), (), s32[]{:S(2)}) async-start(), calls=%async_computation.5 | async-start | bytes 10881024 | tf_op jit(solution)/shard_map/all_gather | solution.py:73
  19.5 130.0 %all-to-all-start = ((bf16[8,2,2,192,512]{4,3,2,1,0:T(8,128)(2,1)}), bf16[8,2,2,192,512]{4,3,2,1,0:T(8,128)(2,1)}, u32[]{:S(2)}, u32[]{:S(2)}) async-start(bf16[8,2,2,192,512]{4,3,2,1,0:T(8,128)(2,1)} %stack.11), calls=%async_computation | async-start | bytes 12582912 | tf_op jit(solution)/shard_map/all_to_all | solution.py:87
  25.9 388.5 %reduce-scatter.3.cloned.1.call-start = ((), (), s32[]{:S(2)}) async-start(), calls=%async_computation.3 | async-start | bytes 7225344 | tf_op jit(solution)/shard_map/reduce_scatter | solution.py:177
  179.0 10.8 %copy-start.18 = (f32[2,192]{1,0:T(2,128)}, f32[2,192]{1,0:T(2,128)S(1)}, u32[]{:S(2)}) copy-start(f32[2,192]{1,0:T(2,128)S(1)} %add_rsqrt_fusion) | copy-start | bytes 4612
  200.2 2.3 copy-start.4
  202.5 1.9 copy-start.1
  240.3 3.1 copy-start.11
  246.4 4.2 copy-start.6
  246.4 4.2 copy-start.15
  251.6 5.9 copy-start.5
  251.6 5.9 copy-start.17
  257.5 4.5 copy-start
  265.9 3.5 copy-start.21
  265.9 3.5 copy-start.22
  265.9 3.5 copy-start.3
  278.0 298.8 %reduce-scatter.5.cloned.1.call-start = ((), (), s32[]{:S(2)}) async-start(), calls=%async_computation.4 | async-start | bytes 11894784 | tf_op jit(solution)/shard_map/reduce_scatter | solution.py:201
  285.3 6.2 %copy-start.13 = (bf16[2,192,512]{2,1,0:T(8,128)(2,1)S(1)}, bf16[2,192,512]{2,1,0:T(8,128)(2,1)}, u32[]{:S(2)}) copy-start(bf16[2,192,512]{2,1,0:T(8,128)(2,1)} %reshape.225) | copy-start | bytes 1179652
  303.6 6.7 %copy-start.2 = (bf16[2,192,32,128]{3,2,1,0:T(8,128)(2,1)S(1)}, bf16[2,192,32,128]{3,2,1,0:T(8,128)(2,1)}, u32[]{:S(2)}) copy-start(bf16[2,192,32,128]{3,2,1,0:T(8,128)(2,1)} %reshape_squeeze.4) | copy-start | bytes 9437188
  303.6 6.7 %copy-start.14 = (bf16[2,192,512,1]{2,1,0,3:T(8,128)(2,1)S(1)}, bf16[2,192,512,1]{2,1,0,3:T(8,128)(2,1)}, u32[]{:S(2)}) copy-start(bf16[2,192,512,1]{2,1,0,3:T(8,128)(2,1)} %reshape.255) | copy-start | bytes 1179652
  314.9 104.9 %copy-start.8 = (bf16[32,128,128]{1,2,0:T(8,128)(2,1)S(1)}, bf16[32,128,128]{1,2,0:T(8,128)(2,1)}, u32[]{:S(2)}) copy-start(bf16[32,128,128]{1,2,0:T(8,128)(2,1)} %copy.100) | copy-start | bytes 3145732
  314.9 104.9 %copy-start.9 = (bf16[32,128,128]{1,2,0:T(8,128)(2,1)S(1)}, bf16[32,128,128]{1,2,0:T(8,128)(2,1)}, u32[]{:S(2)}) copy-start(bf16[32,128,128]{1,2,0:T(8,128)(2,1)} %copy.99) | copy-start | bytes 3145732
  439.4 1.7 copy-start.12
  440.6 1.5 copy-start.20
  440.6 1.5 copy-start.24
  (6 other events, 6.5 us)
Sparse Core Ops, SparseCore 0:
  12.2 117.6 all-gather.2
  278.1 136.2 reduce-scatter.2
  439.5 137.1 reduce-scatter.4
